TPU v7x, 128 devices: a whole 4x4x4 slice. The times are simulated.
128 devices in a mesh: fr: 4 (over x_hi, core), fc: 32 (over z, x_lo, y).
Axes of the slice: x: 4 (x_hi: 2, x_lo: 2; x = x_hi * 2 + x_lo), y: 4, z: 4, core: 2. Of those that a mesh axis runs over, the one named last changes fastest.
Arguments:
- front_slab: float32 [2048, 98304], P('fr', 'fc'), may hold values from -6 to 6
- panels: float32 [4, 98304, 256], P(None, 'fc'), may hold values from -8 to 8
- diagonal_blocks: float32 [4, 256, 256], P(None, None, 'fc'), may hold values from -3 to 96, as said below
- extend_maps: int32 [4, 4, 32, 128], P(None, 'fr', 'fc'), may hold values from 0 to 127, each once within a row
Outputs:
- front_out: float32 [2048, 98304], P('fr', 'fc')
Inputs may be any that keep to these rules, and one draw needn't show every extreme that they name: `extend_maps`: each level's map at each grid position names every row of the block once. `diagonal_blocks`: the symmetric part of each block is positive definite.
All inputs are finite; a program needn't handle non-finite values.
Results may differ from a plain program's by a relative error of at most 0.0001.
Values sent between devices are 32-bit elements; how exact they have to be, the bound alone decides.
No kernel may reach another device: no remote copies, remote signals or barrier semaphores. Data moves between devices by JAX's collectives and lax.ppermute only.
A program may use at most 128 MiB of HBM per device.

v0:
```python
import jax
import jax.numpy as jnp
from jax import lax
from jax.sharding import PartitionSpec as P

HIGHEST = lax.Precision.HIGHEST


def partner(x, axis, distance):
    return lax.ppermute(x, axis, [(i, i ^ 1 << distance) for i in range(lax.axis_size(axis))])


def broadcast(block, axis, source):
    block = jnp.where(lax.axis_index(axis) == source, block, jnp.zeros_like(block))
    return lax.psum(block, axis)


def inverse_factor(diagonal_block):
    symmetric = 0.5 * (diagonal_block + diagonal_block.T)
    lower_factor = jnp.linalg.cholesky(symmetric)
    identity = jnp.eye(symmetric.shape[0], dtype=symmetric.dtype)
    return lax.linalg.triangular_solve(lower_factor, identity, left_side=True, lower=True)


def swap_columns(top_rows, bit_index):
    return partner(top_rows, "fc", bit_index)


def swap_rows(top_rows, bit_index):
    return partner(top_rows, "fr", bit_index)


def merge_top(front_slab, received, row_map):
    block_rows = row_map.shape[0]
    moved_rows = jnp.take(received, row_map, axis=0)
    return lax.dynamic_update_slice(front_slab, front_slab[:block_rows] + moved_rows, (0, 0))


def body(front_slab, panels, diagonal_blocks, extend_maps):
    row_count, col_count = front_slab.shape
    block_rows = extend_maps.shape[3]
    row_index = lax.axis_index("fr")
    row_devices = lax.axis_size("fr")
    col_devices = lax.axis_size("fc")
    whole_diagonal = lax.all_gather(diagonal_blocks, "fc", axis=2, tiled=True)
    partner_plan = [
        (True, col_devices.bit_length() - 2),
        (True, 0),
        (False, row_devices.bit_length() - 2),
        (False, 0),
    ]
    pending = None
    for level_index in range(4):
        use_columns, bit_index = partner_plan[level_index]
        top_rows = front_slab[:block_rows]
        received = (
            swap_columns(top_rows, bit_index) if use_columns else swap_rows(top_rows, bit_index)
        )
        front_slab = merge_top(front_slab, received, extend_maps[level_index, 0, 0])
        inverse = inverse_factor(whole_diagonal[level_index])
        panel_level = panels[level_index]
        column_factor = jnp.dot(panel_level, inverse.T, precision=HIGHEST)
        first_row = row_index * row_count
        source = lax.dynamic_slice_in_dim(column_factor, first_row % col_count, row_count, 0)
        slab_factor = broadcast(source, "fc", first_row // col_count)
        front_slab = front_slab - jnp.dot(slab_factor, column_factor.T, precision=HIGHEST)
    return front_slab


def solution(mesh):
    in_specs = (P("fr", "fc"), P(None, "fc", None), P(None, None, "fc"), P(None, "fr", "fc", None))
    out_specs = P("fr", "fc")
    return jax.shard_map(body, mesh=mesh, in_specs=in_specs, out_specs=out_specs, check_vma=False)
```

profile of v0, /device:TPU:1, one launch (start us, length us, event | category | flops | bytes accessed | tf_op | source)
XLA Modules:
  0.0 866.0 jit_solution(11738925772173782008)
XLA Ops:
  6.5 6.2 copy.97
  13.5 2.8 slice.90
  16.2 4.4 collective-permute-start
  20.7 126.8 %all-gather.2.cloned.1.call-done = f32[4,256,256]{1,0,2:T(4,128)} async-done(((f32[4,256,8]{1,0,2:T(4,128)}), f32[4,256,256]{1,0,2:T(4,128)}) %all-gather.2.cloned.1.call-update) | async-done | bytes 1048592 | tf_op jit(solution)/shard_map/all_gather | solution.py:45
  147.5 3.6 fusion.73
  154.1 11.7 %cholesky.214 = f32[128,128]{1,0:T(8,128)S(1)} custom-call(f32[128,128]{1,0:T(8,128)S(1)} %cholesky.346), custom_call_target="Cholesky" | custom-call | tf_op jit(solution)/shard_map/jit(cholesky)/cholesky | solution.py:20
  165.8 9.8 %custom-call.17 = f32[1,128,128]{1,2,0:T(8,128)S(1)} custom-call(f32[1,128,128]{2,1,0:T(8,128)S(1)} %get-tuple-element.109), custom_call_target="InvertDiagBlocksLowerTriangular" | custom-call | tf_op jit(solution)/shard_map/jit(cholesky)/cholesky | solution.py:20
  176.1 11.7 %cholesky.231 = f32[128,128]{1,0:T(8,128)S(1)} custom-call(f32[128,128]{1,0:T(8,128)S(1)} %convolution_subtract_fusion.11), custom_call_target="Cholesky" | custom-call | tf_op jit(solution)/shard_map/jit(cholesky)/cholesky | solution.py:20
  190.6 4.0 while.8
  194.6 20.0 %custom-call.18 = f32[2,128,128]{1,2,0:T(8,128)S(1)} custom-call(f32[2,128,128]{2,1,0:T(8,128)S(1)} %get-tuple-element.34), custom_call_target="InvertDiagBlocksLowerTriangular" | custom-call | tf_op jit(solution)/shard_map/triangular_solve/custom-call.0 | solution.py:22
  215.7 11.7 %cholesky.248 = f32[128,128]{1,0:T(8,128)S(1)} custom-call(f32[128,128]{1,0:T(8,128)S(1)} %cholesky.349), custom_call_target="Cholesky" | custom-call | tf_op jit(solution)/shard_map/jit(cholesky)/cholesky | solution.py:20
  227.5 9.8 %custom-call.19 = f32[1,128,128]{1,2,0:T(8,128)S(1)} custom-call(f32[1,128,128]{2,1,0:T(8,128)S(1)} %get-tuple-element.105), custom_call_target="InvertDiagBlocksLowerTriangular" | custom-call | tf_op jit(solution)/shard_map/jit(cholesky)/cholesky | solution.py:20
  237.8 11.7 %cholesky.265 = f32[128,128]{1,0:T(8,128)S(1)} custom-call(f32[128,128]{1,0:T(8,128)S(1)} %convolution_subtract_fusion.10), custom_call_target="Cholesky" | custom-call | tf_op jit(solution)/shard_map/jit(cholesky)/cholesky | solution.py:20
  252.3 4.1 while.9
  256.5 19.8 %custom-call.20 = f32[2,128,128]{1,2,0:T(8,128)S(1)} custom-call(f32[2,128,128]{2,1,0:T(8,128)S(1)} %get-tuple-element.35), custom_call_target="InvertDiagBlocksLowerTriangular" | custom-call | tf_op jit(solution)/shard_map/triangular_solve/custom-call.0 | solution.py:22
  277.2 6.4 fusion.6
  283.6 6.3 fusion.4
  290.5 11.7 %cholesky.282 = f32[128,128]{1,0:T(8,128)S(1)} custom-call(f32[128,128]{1,0:T(8,128)S(1)} %cholesky.352), custom_call_target="Cholesky" | custom-call | tf_op jit(solution)/shard_map/jit(cholesky)/cholesky | solution.py:20
  302.3 10.0 %custom-call.21 = f32[1,128,128]{1,2,0:T(8,128)S(1)} custom-call(f32[1,128,128]{2,1,0:T(8,128)S(1)} %get-tuple-element.101), custom_call_target="InvertDiagBlocksLowerTriangular" | custom-call | tf_op jit(solution)/shard_map/jit(cholesky)/cholesky | solution.py:20
  312.8 11.7 %cholesky.299 = f32[128,128]{1,0:T(8,128)S(1)} custom-call(f32[128,128]{1,0:T(8,128)S(1)} %convolution_subtract_fusion.9), custom_call_target="Cholesky" | custom-call | tf_op jit(solution)/shard_map/jit(cholesky)/cholesky | solution.py:20
  327.3 4.2 while.10
  331.5 20.1 %custom-call.22 = f32[2,128,128]{1,2,0:T(8,128)S(1)} custom-call(f32[2,128,128]{2,1,0:T(8,128)S(1)} %get-tuple-element.36), custom_call_target="InvertDiagBlocksLowerTriangular" | custom-call | tf_op jit(solution)/shard_map/triangular_solve/custom-call.0 | solution.py:22
  352.5 6.4 fusion.2
  359.0 11.7 %cholesky.316 = f32[128,128]{1,0:T(8,128)S(1)} custom-call(f32[128,128]{1,0:T(8,128)S(1)} %cholesky.355), custom_call_target="Cholesky" | custom-call | tf_op jit(solution)/shard_map/jit(cholesky)/cholesky | solution.py:20
  370.8 9.8 %custom-call.23 = f32[1,128,128]{1,2,0:T(8,128)S(1)} custom-call(f32[1,128,128]{2,1,0:T(8,128)S(1)} %get-tuple-element.97), custom_call_target="InvertDiagBlocksLowerTriangular" | custom-call | tf_op jit(solution)/shard_map/jit(cholesky)/cholesky | solution.py:20
  381.1 11.9 %cholesky.333 = f32[128,128]{1,0:T(8,128)S(1)} custom-call(f32[128,128]{1,0:T(8,128)S(1)} %convolution_subtract_fusion.8), custom_call_target="Cholesky" | custom-call | tf_op jit(solution)/shard_map/jit(cholesky)/cholesky | solution.py:20
  395.8 4.2 while.11
  396.5 1.4 bitcast_dynamic-update-slice_fusion.11
  400.0 19.7 %custom-call.24 = f32[2,128,128]{1,2,0:T(8,128)S(1)} custom-call(f32[2,128,128]{2,1,0:T(8,128)S(1)} %get-tuple-element.37), custom_call_target="InvertDiagBlocksLowerTriangular" | custom-call | tf_op jit(solution)/shard_map/triangular_solve/custom-call.0 | solution.py:22
  420.6 4.8 fusion
  425.4 2.6 select_bitcast_fusion.3
  428.0 2.1 select_bitcast_fusion.2
  430.1 2.1 select_bitcast_fusion.1
  434.5 2.8 fusion.15
  437.3 308.5 %all-reduce.4.cloned.1.call-done = (f32[512,256]{0,1:T(8,128)}, f32[512,256]{0,1:T(8,128)}, f32[512,256]{0,1:T(8,128)}, f32[512,256]{0,1:T(8,128)}) async-done(((f32[512,256]{0,1:T(8,128)}, f32[512,256]{0,1:T(8,128)}, f32[512,256]{0,1:T(8,128)}, f32[512,256]{0,1:T(8,128)}), (f32[512,256]{0,1:T(8,128)}, f32[512,256]{0,1:T(8,128)}, f32[512,256]{0,1:T(8,128)}, ...) | async-done | bytes 2097168 | tf_op jit(solution)/shard_map/psum | solution.py:15
  745.8 8.1 convolution_subtract_fusion.3
  754.9 1.7 copy-done.1
  756.6 17.6 %collective-permute-done.1 = f32[128,3072]{1,0:T(8,128)S(1)} collective-permute-done((f32[128,3072]{1,0:T(8,128)S(1)}, f32[128,3072]{1,0:T(8,128)S(1)}, u32[]{:S(2)}, u32[]{:S(2)}) %collective-permute-start.1) | collective-permute-done | bytes 1572896 | tf_op jit(solution)/shard_map/ppermute | solution.py:10
  775.4 2.9 fusion.14
  778.3 7.3 convolution_subtract_fusion.2
  785.8 2.5 collective-permute-start.2
  788.4 18.3 %collective-permute-done.2 = f32[128,3072]{1,0:T(8,128)S(1)} collective-permute-done((f32[128,3072]{1,0:T(8,128)S(1)}, f32[128,3072]{1,0:T(8,128)S(1)}, u32[]{:S(2)}, u32[]{:S(2)}) %collective-permute-start.2) | collective-permute-done | bytes 1572896 | tf_op jit(solution)/shard_map/ppermute | solution.py:10
  807.8 2.9 fusion.13
  810.8 7.3 convolution_subtract_fusion.1
  818.2 24.5 %collective-permute-start.3 = (f32[128,3072]{1,0:T(8,128)S(1)}, f32[128,3072]{1,0:T(8,128)S(1)}, u32[]{:S(2)}, u32[]{:S(2)}) collective-permute-start(f32[128,3072]{1,0:T(8,128)S(1)} %slice.182), channel_id=1, source_target_pairs={{0,32},{32,0},{64,96},{96,64},{1,33},{33,1},{65,97},{97,65},{2,34}... | collective-permute-start | bytes 4718600 | tf_op jit(solution)/shard_map/ppermute | solution.py:10
  842.7 3.0 collective-permute-done.3
  846.9 2.9 fusion.12
  849.8 9.0 %convolution_subtract_fusion = f32[512,3072]{1,0:T(8,128)} fusion(f32[512,3072]{1,0:T(8,128)} %fusion.12, f32[512,256]{0,1:T(8,128)S(1)} %copy-done.7, f32[256,3072]{1,0:T(8,128)S(1)} %copy-done.6), kind=kOutput, calls=%fused_computation.12 | convolution fusion | flops 4833411072 | bytes 16252928 | tf_op jit(solution)/shard_map/dot_general | solution.py:66
  (135 shorter events, 38.1 us)
Async XLA Ops:
  6.5 6.3 copy-start.10
  6.5 141.0 %all-gather.2.cloned.1.call-start = ((), (), s32[]{:S(2)}) async-start(), calls=%async_computation | async-start | bytes 1081344 | tf_op jit(solution)/shard_map/all_gather | solution.py:45
  13.4 732.4 %all-reduce.4.cloned.1.call-start = ((), (), s32[]{:S(2)}) async-start(), calls=%async_computation.1 | async-start | bytes 4194304 | tf_op jit(solution)/shard_map/psum | solution.py:15
  16.2 417.1 %collective-permute-start = (f32[128,3072]{1,0:T(8,128)}, f32[128,3072]{1,0:T(8,128)S(1)}, u32[]{:S(2)}, u32[]{:S(2)}) collective-permute-start(f32[128,3072]{1,0:T(8,128)} %slice.90), channel_id=1, source_target_pairs={{0,16},{1,17},{2,18},{3,19},{4,20},{5,21},{6,22},{7,23},{8,24},{9,... | collective-permute-start | bytes 4718600 | tf_op jit(solution)/shard_map/ppermute | solution.py:10
  425.4 6.8 copy-start.5
  425.4 7.9 copy-start.11
  753.9 2.7 copy-start.1
  754.0 20.2 %collective-permute-start.1 = (f32[128,3072]{1,0:T(8,128)S(1)}, f32[128,3072]{1,0:T(8,128)S(1)}, u32[]{:S(2)}, u32[]{:S(2)}) collective-permute-start(f32[128,3072]{1,0:T(8,128)S(1)} %slice.172), channel_id=1, source_target_pairs={{0,1},{1,0},{2,3},{3,2},{4,5},{5,4},{6,7},{7,6},{8,9},{9,8},{10,11... | collective-permute-start | bytes 4718600 | tf_op jit(solution)/shard_map/ppermute | solution.py:10
  775.4 3.0 copy-start.3
  775.4 2.9 copy-start.9
  785.6 2.7 copy-start.2
  785.8 20.9 %collective-permute-start.2 = (f32[128,3072]{1,0:T(8,128)S(1)}, f32[128,3072]{1,0:T(8,128)S(1)}, u32[]{:S(2)}, u32[]{:S(2)}) collective-permute-start(f32[128,3072]{1,0:T(8,128)S(1)} %slice.177), channel_id=1, source_target_pairs={{0,64},{32,96},{64,0},{96,32},{1,65},{33,97},{65,1},{97,33},{2,66}... | collective-permute-start | bytes 4718600 | tf_op jit(solution)/shard_map/ppermute | solution.py:10
  807.8 3.0 copy-start.4
  807.8 2.9 copy-start.8
  818.1 24.6 %copy-start = (f32[512,3072]{1,0:T(8,128)}, f32[512,3072]{1,0:T(8,128)S(1)}, u32[]{:S(2)}) copy-start(f32[512,3072]{1,0:T(8,128)S(1)} %convolution_subtract_fusion.1) | copy-start | bytes 18874372
  818.2 27.5 %collective-permute-start.3 = (f32[128,3072]{1,0:T(8,128)S(1)}, f32[128,3072]{1,0:T(8,128)S(1)}, u32[]{:S(2)}, u32[]{:S(2)}) collective-permute-start(f32[128,3072]{1,0:T(8,128)S(1)} %slice.182), channel_id=1, source_target_pairs={{0,32},{32,0},{64,96},{96,64},{1,33},{33,1},{65,97},{97,65},{2,34}... | collective-permute-start | bytes 4718600 | tf_op jit(solution)/shard_map/ppermute | solution.py:10
  846.9 3.0 copy-start.6
  846.9 2.9 copy-start.7
Sparse Core Ops, SparseCore 0:
  13.5 133.9 all-gather.1
  433.4 312.3 all-reduce.3
where the time goes:
time: 877 us; the launch traced here: 866 us
  waiting for transfers between devices  474 us (54%)
  other arithmetic  240 us (27%)
  matrix products  61 us (7%)
  local copies, waits for them, and re-layouts  38.9 us (4%)
  starting transfers between devices  32.4 us (4%)
  between operations  19.6 us (2%)
    psum x1, waiting for transfers between devices, broadcast(): return lax.psum(block, axis)  308 us
    another operation x28, other arithmetic, inverse_factor(): lower_factor = jnp.linalg.cholesky(symmetric)  139 us
    all_gather x1, waiting for transfers between devices, body(): whole_diagonal = lax.all_gather(diagonal_blocks, 'fc', axis=2, tiled=True)  127 us
    another operation x9, other arithmetic, inverse_factor(): lax.linalg.triangular_solve(lower_factor, identity, left_side=True, lower...  79.7 us
    ppermute x4, waiting for transfers between devices, partner(): lax.ppermute(x, axis, [(i, i ^ 1 << distance) for i in range(lax.axis_siz...  38.9 us
    ppermute x4, starting transfers between devices, partner(): lax.ppermute(x, axis, [(i, i ^ 1 << distance) for i in range(lax.axis_siz...  32.3 us
    dot_general x4, matrix products, body(): jnp.dot(slab_factor, column_factor.T, precision=HIGHEST)  31.7 us
    dot_general x4, matrix products, body(): column_factor = jnp.dot(panel_level, inverse.T, precision=HIGHEST)  23.9 us
  transfers between devices with their start and end apart: 6, of which 5 were waited for; matrix products, arithmetic and copies ran while one was open for 33% of the time, Pallas kernels for 0%

commit v1 on v0

--- a/solution.py
+++ b/solution.py
@@ -42,7 +42,9 @@
     row_index = lax.axis_index("fr")
     row_devices = lax.axis_size("fr")
     col_devices = lax.axis_size("fc")
-    whole_diagonal = lax.all_gather(diagonal_blocks, "fc", axis=2, tiled=True)
+    whole_diagonal = jnp.concatenate(
+        lax.all_to_all(jnp.stack([diagonal_blocks] * lax.axis_size("fc")), "fc", 0, 0), axis=2
+    )
     partner_plan = [
         (True, col_devices.bit_length() - 2),
         (True, 0),

time: 877 us -> 788 us (0.90)
  waiting for transfers between devices: 474 us -> 367 us
  starting transfers between devices: 32.4 us -> 41.3 us
    all_gather x1 -> x0, waiting for transfers between devices: 127 us -> none  [body(): whole_diagonal = lax.all_gather(diagonal_blocks, 'fc', axis=2, tiled=True)]
    psum x1, waiting for transfers between devices: 308 us -> 319 us  [broadcast(): return lax.psum(block, axis)]
    all_to_all x0 -> x1, waiting for transfers between devices: none -> 9.99 us  [body(): lax.all_to_all(jnp.stack([diagonal_blocks] * lax.axis_size('fc')), 'fc',...]
    all_to_all x0 -> x1, starting transfers between devices: none -> 9.94 us  [body(): lax.all_to_all(jnp.stack([diagonal_blocks] * lax.axis_size('fc')), 'fc',...]
  transfers between devices with their start and end apart: 6 -> 6, of which waited for: 5 -> 5; matrix products, arithmetic and copies ran while one was open for 33% -> 38% of each run, Pallas kernels for 0% -> 0%
where the time goes in v1:
time: 788 us; the launch traced here: 776 us
  waiting for transfers between devices  367 us (47%)
  other arithmetic  242 us (31%)
  matrix products  62.5 us (8%)
  local copies, waits for them, and re-layouts  43.6 us (6%)
  starting transfers between devices  41.3 us (5%)
  between operations  19.6 us (2%)
    psum x1, waiting for transfers between devices, broadcast(): return lax.psum(block, axis)  319 us
    another operation x28, other arithmetic, inverse_factor(): lower_factor = jnp.linalg.cholesky(symmetric)  139 us
    another operation x9, other arithmetic, inverse_factor(): lax.linalg.triangular_solve(lower_factor, identity, left_side=True, lower...  79.7 us
    ppermute x4, waiting for transfers between devices, partner(): lax.ppermute(x, axis, [(i, i ^ 1 << distance) for i in range(lax.axis_siz...  38.6 us
    dot_general x4, matrix products, body(): jnp.dot(slab_factor, column_factor.T, precision=HIGHEST)  31.5 us
    ppermute x4, starting transfers between devices, partner(): lax.ppermute(x, axis, [(i, i ^ 1 << distance) for i in range(lax.axis_siz...  31.3 us
    dot_general x4, matrix products, body(): column_factor = jnp.dot(panel_level, inverse.T, precision=HIGHEST)  23.9 us
    another operation x29, local copies, waits for them, and re-layouts, inverse_factor(): lax.linalg.triangular_solve(lower_factor, identity, left_side=True, lower...  16.4 us
  transfers between devices with their start and end apart: 6, of which 5 were waited for; matrix products, arithmetic and copies ran while one was open for 38% of the time, Pallas kernels for 0%

profile of v1, /device:TPU:1, one launch (start us, length us, event | category | flops | bytes accessed | tf_op | source)
XLA Modules:
  0.0 776.1 jit_solution(1642201781443966199)
XLA Ops:
  6.5 6.2 copy.82
  13.9 9.9 %all-to-all-start = ((f32[32,4,256,8]{2,3,1,0:T(8,128)}), f32[32,4,256,8]{2,3,1,0:T(8,128)}, u32[]{:S(2)}, u32[]{:S(2)}) async-start(f32[32,4,256,8]{2,3,1,0:T(8,128)} %stack.2), calls=%async_computation | async-start | bytes 2097152 | tf_op jit(solution)/shard_map/all_to_all | solution.py:46
  23.9 2.8 slice.94
  26.7 2.7 collective-permute-start
  29.4 10.0 %all-to-all-done = f32[32,4,256,8]{2,3,1,0:T(8,128)} async-done(((f32[32,4,256,8]{2,3,1,0:T(8,128)}), f32[32,4,256,8]{2,3,1,0:T(8,128)}, u32[]{:S(2)}, u32[]{:S(2)}) %all-to-all-start) | async-done | bytes 1048608 | tf_op jit(solution)/shard_map/all_to_all | solution.py:46
  43.3 1.8 copy.27
  46.8 2.1 fusion.29
  52.9 11.7 %cholesky.214 = f32[128,128]{1,0:T(8,128)S(1)} custom-call(f32[128,128]{1,0:T(8,128)S(1)} %cholesky.346), custom_call_target="Cholesky" | custom-call | tf_op jit(solution)/shard_map/jit(cholesky)/cholesky | solution.py:20
  64.6 9.8 %custom-call.17 = f32[1,128,128]{1,2,0:T(8,128)S(1)} custom-call(f32[1,128,128]{2,1,0:T(8,128)S(1)} %get-tuple-element.113), custom_call_target="InvertDiagBlocksLowerTriangular" | custom-call | tf_op jit(solution)/shard_map/jit(cholesky)/cholesky | solution.py:20
  76.6 11.7 %cholesky.231 = f32[128,128]{1,0:T(8,128)S(1)} custom-call(f32[128,128]{1,0:T(8,128)S(1)} %convolution_subtract_fusion.11), custom_call_target="Cholesky" | custom-call | tf_op jit(solution)/shard_map/jit(cholesky)/cholesky | solution.py:20
  91.1 4.0 while.8
  95.1 20.0 %custom-call.18 = f32[2,128,128]{1,2,0:T(8,128)S(1)} custom-call(f32[2,128,128]{2,1,0:T(8,128)S(1)} %get-tuple-element.34), custom_call_target="InvertDiagBlocksLowerTriangular" | custom-call | tf_op jit(solution)/shard_map/triangular_solve/custom-call.0 | solution.py:22
  116.0 11.7 %cholesky.248 = f32[128,128]{1,0:T(8,128)S(1)} custom-call(f32[128,128]{1,0:T(8,128)S(1)} %cholesky.349), custom_call_target="Cholesky" | custom-call | tf_op jit(solution)/shard_map/jit(cholesky)/cholesky | solution.py:20
  127.8 9.8 %custom-call.19 = f32[1,128,128]{1,2,0:T(8,128)S(1)} custom-call(f32[1,128,128]{2,1,0:T(8,128)S(1)} %get-tuple-element.109), custom_call_target="InvertDiagBlocksLowerTriangular" | custom-call | tf_op jit(solution)/shard_map/jit(cholesky)/cholesky | solution.py:20
  138.1 11.7 %cholesky.265 = f32[128,128]{1,0:T(8,128)S(1)} custom-call(f32[128,128]{1,0:T(8,128)S(1)} %convolution_subtract_fusion.10), custom_call_target="Cholesky" | custom-call | tf_op jit(solution)/shard_map/jit(cholesky)/cholesky | solution.py:20
  152.6 4.1 while.9
  156.8 19.8 %custom-call.20 = f32[2,128,128]{1,2,0:T(8,128)S(1)} custom-call(f32[2,128,128]{2,1,0:T(8,128)S(1)} %get-tuple-element.35), custom_call_target="InvertDiagBlocksLowerTriangular" | custom-call | tf_op jit(solution)/shard_map/triangular_solve/custom-call.0 | solution.py:22
  177.5 6.4 fusion.6
  183.9 6.3 fusion.4
  190.6 11.7 %cholesky.282 = f32[128,128]{1,0:T(8,128)S(1)} custom-call(f32[128,128]{1,0:T(8,128)S(1)} %cholesky.352), custom_call_target="Cholesky" | custom-call | tf_op jit(solution)/shard_map/jit(cholesky)/cholesky | solution.py:20
  202.4 10.0 %custom-call.21 = f32[1,128,128]{1,2,0:T(8,128)S(1)} custom-call(f32[1,128,128]{2,1,0:T(8,128)S(1)} %get-tuple-element.105), custom_call_target="InvertDiagBlocksLowerTriangular" | custom-call | tf_op jit(solution)/shard_map/jit(cholesky)/cholesky | solution.py:20
  212.9 11.7 %cholesky.299 = f32[128,128]{1,0:T(8,128)S(1)} custom-call(f32[128,128]{1,0:T(8,128)S(1)} %convolution_subtract_fusion.9), custom_call_target="Cholesky" | custom-call | tf_op jit(solution)/shard_map/jit(cholesky)/cholesky | solution.py:20
  227.4 4.2 while.10
  231.6 20.1 %custom-call.22 = f32[2,128,128]{1,2,0:T(8,128)S(1)} custom-call(f32[2,128,128]{2,1,0:T(8,128)S(1)} %get-tuple-element.36), custom_call_target="InvertDiagBlocksLowerTriangular" | custom-call | tf_op jit(solution)/shard_map/triangular_solve/custom-call.0 | solution.py:22
  252.6 6.4 fusion.2
  259.0 11.7 %cholesky.316 = f32[128,128]{1,0:T(8,128)S(1)} custom-call(f32[128,128]{1,0:T(8,128)S(1)} %cholesky.355), custom_call_target="Cholesky" | custom-call | tf_op jit(solution)/shard_map/jit(cholesky)/cholesky | solution.py:20
  270.7 9.8 %custom-call.23 = f32[1,128,128]{1,2,0:T(8,128)S(1)} custom-call(f32[1,128,128]{2,1,0:T(8,128)S(1)} %get-tuple-element.101), custom_call_target="InvertDiagBlocksLowerTriangular" | custom-call | tf_op jit(solution)/shard_map/jit(cholesky)/cholesky | solution.py:20
  281.0 11.9 %cholesky.333 = f32[128,128]{1,0:T(8,128)S(1)} custom-call(f32[128,128]{1,0:T(8,128)S(1)} %convolution_subtract_fusion.8), custom_call_target="Cholesky" | custom-call | tf_op jit(solution)/shard_map/jit(cholesky)/cholesky | solution.py:20
  295.7 4.2 while.11
  299.9 19.7 %custom-call.24 = f32[2,128,128]{1,2,0:T(8,128)S(1)} custom-call(f32[2,128,128]{2,1,0:T(8,128)S(1)} %get-tuple-element.37), custom_call_target="InvertDiagBlocksLowerTriangular" | custom-call | tf_op jit(solution)/shard_map/triangular_solve/custom-call.0 | solution.py:22
  320.5 4.8 fusion
  325.4 2.6 select_bitcast_fusion.3
  328.0 2.1 select_bitcast_fusion.2
  330.1 2.1 select_bitcast_fusion.1
  334.4 2.8 fusion.15
  337.2 318.6 %all-reduce.4.cloned.1.call-done = (f32[512,256]{0,1:T(8,128)}, f32[512,256]{0,1:T(8,128)}, f32[512,256]{0,1:T(8,128)}, f32[512,256]{0,1:T(8,128)}) async-done(((f32[512,256]{0,1:T(8,128)}, f32[512,256]{0,1:T(8,128)}, f32[512,256]{0,1:T(8,128)}, f32[512,256]{0,1:T(8,128)}), (f32[512,256]{0,1:T(8,128)}, f32[512,256]{0,1:T(8,128)}, f32[512,256]{0,1:T(8,128)}, ...) | async-done | bytes 2097168 | tf_op jit(solution)/shard_map/psum | solution.py:15
  655.9 7.9 %convolution_subtract_fusion.3 = f32[512,3072]{1,0:T(8,128)S(1)} fusion(f32[512,3072]{1,0:T(8,128)} %fusion.15, f32[512,256]{0,1:T(8,128)} %get-tuple-element.70, f32[256,3072]{1,0:T(8,128)} %fusion.6), kind=kOutput, calls=%fused_computation.15 | convolution fusion | flops 4833411072 | bytes 16252928 | tf_op jit(solution)/shard_map/dot_general | solution.py:68
  666.5 17.8 %collective-permute-done.1 = f32[128,3072]{1,0:T(8,128)S(1)} collective-permute-done((f32[128,3072]{1,0:T(8,128)S(1)}, f32[128,3072]{1,0:T(8,128)S(1)}, u32[]{:S(2)}, u32[]{:S(2)}) %collective-permute-start.1) | collective-permute-done | bytes 1572896 | tf_op jit(solution)/shard_map/ppermute | solution.py:10
  685.5 2.9 fusion.14
  688.4 7.3 convolution_subtract_fusion.2
  695.8 3.2 collective-permute-start.2
  699.0 17.8 %collective-permute-done.2 = f32[128,3072]{1,0:T(8,128)S(1)} collective-permute-done((f32[128,3072]{1,0:T(8,128)S(1)}, f32[128,3072]{1,0:T(8,128)S(1)}, u32[]{:S(2)}, u32[]{:S(2)}) %collective-permute-start.2) | collective-permute-done | bytes 1572896 | tf_op jit(solution)/shard_map/ppermute | solution.py:10
  718.0 2.9 fusion.13
  721.0 7.3 convolution_subtract_fusion.1
  728.4 24.3 %collective-permute-start.3 = (f32[128,3072]{1,0:T(8,128)S(1)}, f32[128,3072]{1,0:T(8,128)S(1)}, u32[]{:S(2)}, u32[]{:S(2)}) collective-permute-start(f32[128,3072]{1,0:T(8,128)S(1)} %slice.186), channel_id=1, source_target_pairs={{0,32},{32,0},{64,96},{96,64},{1,33},{33,1},{65,97},{97,65},{2,34}... | collective-permute-start | bytes 4718600 | tf_op jit(solution)/shard_map/ppermute | solution.py:10
  752.7 3.0 collective-permute-done.3
  757.0 2.9 fusion.12
  759.9 9.0 %convolution_subtract_fusion = f32[512,3072]{1,0:T(8,128)} fusion(f32[512,3072]{1,0:T(8,128)} %fusion.12, f32[512,256]{0,1:T(8,128)S(1)} %copy-done.8, f32[256,3072]{1,0:T(8,128)S(1)} %copy-done.6), kind=kOutput, calls=%fused_computation.12 | convolution fusion | flops 4833411072 | bytes 16252928 | tf_op jit(solution)/shard_map/dot_general | solution.py:68
  (134 shorter events, 49.4 us)
Async XLA Ops:
  6.5 6.2 copy-start.11
  13.9 25.4 %all-to-all-start = ((f32[32,4,256,8]{2,3,1,0:T(8,128)}), f32[32,4,256,8]{2,3,1,0:T(8,128)}, u32[]{:S(2)}, u32[]{:S(2)}) async-start(f32[32,4,256,8]{2,3,1,0:T(8,128)} %stack.2), calls=%async_computation | async-start | bytes 2097152 | tf_op jit(solution)/shard_map/all_to_all | solution.py:46
  23.9 632.0 %all-reduce.4.cloned.1.call-start = ((), (), s32[]{:S(2)}) async-start(), calls=%async_computation.1 | async-start | bytes 4194304 | tf_op jit(solution)/shard_map/psum | solution.py:15
  26.7 306.6 %collective-permute-start = (f32[128,3072]{1,0:T(8,128)}, f32[128,3072]{1,0:T(8,128)S(1)}, u32[]{:S(2)}, u32[]{:S(2)}) collective-permute-start(f32[128,3072]{1,0:T(8,128)} %slice.94), channel_id=1, source_target_pairs={{0,16},{1,17},{2,18},{3,19},{4,20},{5,21},{6,22},{7,23},{8,24},{9,... | collective-permute-start | bytes 4718600 | tf_op jit(solution)/shard_map/ppermute | solution.py:10
  52.2 0.7 copy-start.7
  325.3 6.8 copy-start.5
  325.4 7.9 %copy-start.12 = (s32[4,1,1,128]{3,2,1,0:T(1,128)S(1)}, s32[4,1,1,128]{3,2,1,0:T(1,128)}, u32[]{:S(2)}) copy-start(s32[4,1,1,128]{3,2,1,0:T(1,128)} %param.12) | copy-start | bytes 6148
  663.8 2.7 copy-start.1
  663.9 20.4 %collective-permute-start.1 = (f32[128,3072]{1,0:T(8,128)S(1)}, f32[128,3072]{1,0:T(8,128)S(1)}, u32[]{:S(2)}, u32[]{:S(2)}) collective-permute-start(f32[128,3072]{1,0:T(8,128)S(1)} %slice.176), channel_id=1, source_target_pairs={{0,1},{1,0},{2,3},{3,2},{4,5},{5,4},{6,7},{7,6},{8,9},{9,8},{10,11... | collective-permute-start | bytes 4718600 | tf_op jit(solution)/shard_map/ppermute | solution.py:10
  685.5 3.0 copy-start.3
  685.5 2.9 copy-start.10
  695.7 3.3 copy-start.2
  695.8 21.0 %collective-permute-start.2 = (f32[128,3072]{1,0:T(8,128)S(1)}, f32[128,3072]{1,0:T(8,128)S(1)}, u32[]{:S(2)}, u32[]{:S(2)}) collective-permute-start(f32[128,3072]{1,0:T(8,128)S(1)} %slice.181), channel_id=1, source_target_pairs={{0,64},{32,96},{64,0},{96,32},{1,65},{33,97},{65,1},{97,33},{2,66}... | collective-permute-start | bytes 4718600 | tf_op jit(solution)/shard_map/ppermute | solution.py:10
  718.0 3.0 copy-start.4
  718.0 2.9 copy-start.9
  728.3 24.4 %copy-start = (f32[512,3072]{1,0:T(8,128)}, f32[512,3072]{1,0:T(8,128)S(1)}, u32[]{:S(2)}) copy-start(f32[512,3072]{1,0:T(8,128)S(1)} %convolution_subtract_fusion.1) | copy-start | bytes 18874372
  728.4 27.3 %collective-permute-start.3 = (f32[128,3072]{1,0:T(8,128)S(1)}, f32[128,3072]{1,0:T(8,128)S(1)}, u32[]{:S(2)}, u32[]{:S(2)}) collective-permute-start(f32[128,3072]{1,0:T(8,128)S(1)} %slice.186), channel_id=1, source_target_pairs={{0,32},{32,0},{64,96},{96,64},{1,33},{33,1},{65,97},{97,65},{2,34}... | collective-permute-start | bytes 4718600 | tf_op jit(solution)/shard_map/ppermute | solution.py:10
  756.9 3.0 copy-start.6
  756.9 2.9 copy-start.8
Sparse Core Ops, SparseCore 0:
  333.3 322.4 all-reduce.3
